TPU v7x, 128 devices: a whole 4x4x4 slice. The times are simulated.
128 devices in a mesh: mem: 16 (over z, y), cell: 8 (over x, core).
Axes of the slice: x: 4, y: 4, z: 4, core: 2. Of those that a mesh axis runs over, the one named last changes fastest.
Arguments:
- turnover_effect: float32 [1024, 65536], P('mem', 'cell'), may hold values from -3 to 3
- base_rate: float32 [65536], P('cell'), may hold values from 0.05 to 0.5
- fast_rate: float32 [65536], P('cell'), may hold values from 0.02 to 0.2
- slow_rate: float32 [65536], P('cell'), may hold values from 0.005 to 0.05
- init_pools: float32 [3, 65536], P(None, 'cell'), may hold values from 1 to 6
- litterfall: float32 [6, 65536], P(None, 'cell'), may hold values from 0.1 to 1
- obs_taps: int32 [16384, 4], P('cell'), may hold values from 0 to 127
- obs_weights: float32 [16384, 4], P('cell'), may hold values from 0.05 to 0.5
- observed: float32 [16384], P('cell'), may hold values from 0.5 to 4
- obs_var: float32 [16384], P('cell'), may hold values from 0.008 to 0.11, as said below
- obs_noise: float32 [1024, 16384], P('mem', 'cell'), may hold values from -6 to 6
Outputs:
- updated_effect: float32 [1024, 65536], P('mem', 'cell')
Inputs may be any that keep to these rules, and one draw needn't show every extreme that they name: `obs_var`: positive variances.
All inputs are finite; a program needn't handle non-finite values.
Results may differ from a plain program's by a relative error of at most 0.00025.
Values sent between devices are 32-bit elements; how exact they have to be, the bound alone decides.
No kernel may reach another device: no remote copies, remote signals or barrier semaphores. Data moves between devices by JAX's collectives and lax.ppermute only.
A program may use at most 192 MiB of HBM per device.

v0:
```python
import math
import jax
import jax.numpy as jnp
from jax import lax
from jax.sharding import PartitionSpec as P

STEPS = 6
BLOCK = 128
TAPS = 4
highest = lax.Precision.HIGHEST


def forward(turnover_effect, base_rate, fast_rate, slow_rate, init_pools, litterfall):
    decayed = 1.0 - jnp.exp(-base_rate[None, :] * jnp.exp(turnover_effect))
    litter = jnp.broadcast_to(init_pools[0][None, :], turnover_effect.shape)
    fast_pool = jnp.broadcast_to(init_pools[1][None, :], turnover_effect.shape)
    slow_pool = jnp.broadcast_to(init_pools[2][None, :], turnover_effect.shape)
    resp_total = jnp.zeros(turnover_effect.shape, jnp.float32)
    for month in range(STEPS):
        litter_out = decayed * litter
        fast_out = fast_rate[None, :] * fast_pool
        slow_out = slow_rate[None, :] * slow_pool
        resp_total = resp_total + 0.6 * litter_out + 0.7 * fast_out + slow_out
        litter = litter - litter_out + litterfall[month][None, :]
        fast_pool = fast_pool + 0.4 * litter_out - fast_out
        slow_pool = slow_pool + 0.3 * fast_out - slow_out
    return resp_total


def observe(resp_total, obs_taps, obs_weights):
    member_count = resp_total.shape[0]
    block_count = resp_total.shape[1] // BLOCK
    positions = jnp.arange(BLOCK, dtype=jnp.int32)
    operator_table = jnp.zeros((obs_taps.shape[0], BLOCK), jnp.float32)
    for tap_index in range(TAPS):
        hits = (obs_taps[:, tap_index][:, None] == positions[None, :]).astype(jnp.float32)
        operator_table = operator_table + obs_weights[:, tap_index][:, None] * hits
    operator_table = operator_table.reshape(block_count, -1, BLOCK)
    blocked = resp_total.reshape(member_count, block_count, BLOCK)
    predicted = jnp.einsum("jbc,boc->jbo", blocked, operator_table, precision=highest)
    return predicted.reshape(member_count, -1)


def spd_solve(matrix, right_side):
    factor = jnp.linalg.cholesky(matrix)
    halfway = lax.linalg.triangular_solve(factor, right_side, left_side=True, lower=True)
    return lax.linalg.triangular_solve(
        factor, halfway, left_side=True, lower=True, transpose_a=True
    )


def contract_last(left, right):
    return lax.dot_general(left, right, (((1,), (1,)), ((), ())), precision=highest)


def body(
    turnover_effect,
    base_rate,
    fast_rate,
    slow_rate,
    init_pools,
    litterfall,
    obs_taps,
    obs_weights,
    observed,
    obs_var,
    obs_noise,
):
    resp_total = forward(turnover_effect, base_rate, fast_rate, slow_rate, init_pools, litterfall)
    predicted = observe(resp_total, obs_taps, obs_weights)
    mem_count = lax.axis_size("mem")
    cell_count = lax.axis_size("cell")
    local_members, local_cells = turnover_effect.shape
    local_obs = predicted.shape[1]
    member_count = local_members * mem_count
    all_obs = local_obs * cell_count
    inv_root = 1.0 / math.sqrt(member_count - 1)
    effect_sum, predicted_sum = lax.psum(
        (jnp.sum(turnover_effect, axis=0), jnp.sum(predicted, axis=0)), "mem"
    )
    anomaly = (turnover_effect - (effect_sum / member_count)[None, :]) * inv_root
    pred_anomaly = (predicted - (predicted_sum / member_count)[None, :]) * inv_root
    residual = observed[None, :] - predicted
    misfit_local = jnp.sum(residual * residual / obs_var[None, :])
    departure = observed[None, :] + jnp.sqrt(obs_var)[None, :] * obs_noise - predicted
    identity_matrix = jnp.eye(member_count, dtype=jnp.float32)
    misfit_sum = lax.psum(misfit_local, ("mem", "cell"))
    stacked = jnp.concatenate(
        [pred_anomaly / obs_var[None, :], departure / obs_var[None, :]], axis=0
    )
    partial_cols = contract_last(lax.all_gather(pred_anomaly, "mem", axis=0, tiled=True), stacked)
    summed = lax.psum(partial_cols, "cell")
    gram = lax.all_gather(summed[:, :local_members], "mem", axis=1, tiled=True)
    step_size = member_count * all_obs / misfit_sum
    local_solve = spd_solve(
        identity_matrix + step_size * gram, step_size * summed[:, local_members:]
    )
    change = jnp.einsum(
        "kj,kc->jc",
        local_solve,
        lax.all_gather(anomaly, "mem", axis=0, tiled=True),
        precision=highest,
    )
    return turnover_effect + change


def solution(mesh):
    in_specs = (
        P("mem", "cell"),
        P("cell"),
        P("cell"),
        P("cell"),
        P(None, "cell"),
        P(None, "cell"),
        P("cell", None),
        P("cell", None),
        P("cell"),
        P("cell"),
        P("mem", "cell"),
    )
    out_specs = P("mem", "cell")
    return jax.shard_map(body, mesh=mesh, in_specs=in_specs, out_specs=out_specs, check_vma=False)
```

profile of v0, /device:TPU:1, one launch (start us, length us, event | category | flops | bytes accessed | tf_op | source)
XLA Modules:
  0.0 692.4 jit_solution(13496281260930924091)
XLA Ops:
  17.2 7.3 %fusion.138 = (f32[8192]{0:T(1024)S(1)}, f32[8,64,8,128]{3,2,1,0:T(8,128)S(1)}) fusion(f32[64,8192]{1,0:T(8,128)} %param.11, f32[8192]{0:T(1024)S(1)} %bitcast.164, f32[8192]{0:T(1024)S(1)} %bitcast.165, f32[8192]{0:T(1024)S(1)} %bitcast.162, f32[8192]{0:T(1024)S(1)} %add_subtract_fusion, f32[8192]{0:T(1024)} %param.14, f32[8192]{0:T(1024)S(1)} %bitcast.163, ...), kind=kLoop, calls=%fused_computation.288 | loop fusion | flops 43507712 | bytes 4718592 | tf_op jit(solution)/shard_map/reduce_sum | solution.py:79
  24.5 9.8 %fusion.32 = (f32[]{:T(128)}, f32[64,32]{1,0:T(8,128)S(1)}, f32[64,32,64]{2,1,0:T(8,128)S(1)}) fusion(f32[64,32]{1,0:T(8,128)S(1)} %div.48, f32[64,32]{1,0:T(8,128)S(1)} %sub.84, f32[8,64,8,128]{3,2,1,0:T(8,128)S(1)} %get-tuple-element.42, f32[64,32]{1,0:T(8,128)S(1)} %mul.268, s32[64,32]{1,0:T(8,128)S(1)} %eq.80, f32[64,32]{1,0:T(8,128)S(1)} %mul.265, ...), kind=kOutput, calls=%fused_computation.81 | convolution fusion | flops 204863488 | bytes 2711556 | tf_op jit(solution)/shard_map/jbc,boc->jbo/dot_general | solution.py:40
  34.3 62.6 %all-reduce.1 = (f32[2048]{0:T(1024)S(1)}, f32[8192]{0:T(1024)S(1)}) all-reduce(f32[2048]{0:T(1024)S(1)} %reduce_sum.31, f32[8192]{0:T(1024)S(1)} %get-tuple-element.41), channel_id=1, replica_groups=mesh['mem'=16,'cell'=8] {'mem'}, use_global_device_ids=true, to_apply=%region_3.0 | all-reduce | flops 10240 | bytes 81920 | tf_op jit(solution)/shard_map/psum | solution.py:78
  99.4 81.4 %all-gather.4.cloned.1.call-done = f32[1024,2048]{1,0:T(8,128)} async-done(((f32[64,2048]{1,0:T(8,128)}), f32[1024,2048]{1,0:T(8,128)}) %all-gather.4.cloned.1.call-update) | async-done | bytes 8388624 | tf_op jit(solution)/shard_map/all_gather | solution.py:91
  180.8 12.0 %fusion.19 = f32[1024,128]{0,1:T(8,128)} fusion(f32[1024,2048]{1,0:T(8,128)} %all-gather.4.cloned.1.call-done, f32[64,2048]{1,0:T(8,128)S(1)} %get-tuple-element.43, f32[64,2048]{1,0:T(8,128)S(1)} %get-tuple-element.33), kind=kOutput, calls=%fused_computation.62 | convolution fusion | flops 3221487616 | bytes 9961472 | tf_op jit(solution)/shard_map/dot_general | solution.py:53
  192.9 64.7 %psum.28 = f32[]{:T(128)} all-reduce(f32[]{:T(128)} %get-tuple-element.13), channel_id=1, replica_groups=mesh['mem'=16,'cell'=8] {'mem','cell'}, use_global_device_ids=true, to_apply=%region_1.0 | all-reduce | flops 1 | bytes 8 | tf_op jit(solution)/shard_map/psum | solution.py:87
  261.8 47.4 %all-gather.6.cloned.1.call-done = f32[1024,1024]{0,1:T(8,128)} async-done(((f32[1024,64]{0,1:T(8,128)}), f32[1024,1024]{0,1:T(8,128)}) %all-gather.6.cloned.1.call-update) | async-done | bytes 4194320 | tf_op jit(solution)/shard_map/all_gather | solution.py:93
  309.1 4.9 multiply_add_fusion
  314.1 5.8 copy.21
  319.9 5.7 fusion
  327.7 11.7 %cholesky.223 = f32[128,128]{1,0:T(8,128)S(1)} custom-call(f32[128,128]{1,0:T(8,128)S(1)} %cholesky.580), custom_call_target="Cholesky" | custom-call | tf_op jit(solution)/shard_map/jit(cholesky)/cholesky | solution.py:45
  339.4 2.5 cholesky.255
  341.9 9.8 %custom-call.64 = f32[1,128,128]{1,2,0:T(8,128)S(1)} custom-call(f32[1,128,128]{2,1,0:T(8,128)S(1)} %get-tuple-element.75), custom_call_target="InvertDiagBlocksLowerTriangular" | custom-call | tf_op jit(solution)/shard_map/jit(cholesky)/cholesky | solution.py:45
  355.6 11.8 %cholesky.244 = f32[128,128]{1,0:T(8,128)S(1)} custom-call(f32[128,128]{1,0:T(8,128)S(1)} %cholesky.584), custom_call_target="Cholesky" | custom-call | tf_op jit(solution)/shard_map/jit(cholesky)/cholesky | solution.py:45
  368.1 9.8 %custom-call.65 = f32[1,128,128]{1,2,0:T(8,128)S(1)} custom-call(f32[1,128,128]{2,1,0:T(8,128)S(1)} %get-tuple-element.72), custom_call_target="InvertDiagBlocksLowerTriangular" | custom-call | tf_op jit(solution)/shard_map/jit(cholesky)/cholesky | solution.py:45
  381.3 11.7 %cholesky.468 = f32[128,128]{1,0:T(8,128)S(1)} custom-call(f32[128,128]{1,0:T(8,128)S(1)} %cholesky.589), custom_call_target="Cholesky" | custom-call | tf_op jit(solution)/shard_map/jit(cholesky)/cholesky | solution.py:45
  393.6 9.8 %custom-call.66 = f32[1,128,128]{1,2,0:T(8,128)S(1)} custom-call(f32[1,128,128]{2,1,0:T(8,128)S(1)} %get-tuple-element.69), custom_call_target="InvertDiagBlocksLowerTriangular" | custom-call | tf_op jit(solution)/shard_map/jit(cholesky)/cholesky | solution.py:45
  404.6 2.3 convolution_subtract_fusion.2
  407.0 11.9 %cholesky.487 = f32[128,128]{1,0:T(8,128)S(1)} custom-call(f32[128,128]{1,0:T(8,128)S(1)} %cholesky.594), custom_call_target="Cholesky" | custom-call | tf_op jit(solution)/shard_map/jit(cholesky)/cholesky | solution.py:45
  419.5 9.8 %custom-call.67 = f32[1,128,128]{1,2,0:T(8,128)S(1)} custom-call(f32[1,128,128]{2,1,0:T(8,128)S(1)} %get-tuple-element.66), custom_call_target="InvertDiagBlocksLowerTriangular" | custom-call | tf_op jit(solution)/shard_map/jit(cholesky)/cholesky | solution.py:45
  430.5 2.4 convolution_subtract_fusion.3
  432.9 11.7 %cholesky.506 = f32[128,128]{1,0:T(8,128)S(1)} custom-call(f32[128,128]{1,0:T(8,128)S(1)} %cholesky.599), custom_call_target="Cholesky" | custom-call | tf_op jit(solution)/shard_map/jit(cholesky)/cholesky | solution.py:45
  445.2 10.2 %custom-call.68 = f32[1,128,128]{1,2,0:T(8,128)S(1)} custom-call(f32[1,128,128]{2,1,0:T(8,128)S(1)} %get-tuple-element.63), custom_call_target="InvertDiagBlocksLowerTriangular" | custom-call | tf_op jit(solution)/shard_map/jit(cholesky)/cholesky | solution.py:45
  458.8 11.7 %cholesky.526 = f32[128,128]{1,0:T(8,128)S(1)} custom-call(f32[128,128]{1,0:T(8,128)S(1)} %cholesky.604), custom_call_target="Cholesky" | custom-call | tf_op jit(solution)/shard_map/jit(cholesky)/cholesky | solution.py:45
  471.2 9.8 %custom-call.69 = f32[1,128,128]{1,2,0:T(8,128)S(1)} custom-call(f32[1,128,128]{2,1,0:T(8,128)S(1)} %get-tuple-element.60), custom_call_target="InvertDiagBlocksLowerTriangular" | custom-call | tf_op jit(solution)/shard_map/jit(cholesky)/cholesky | solution.py:45
  484.0 11.9 %cholesky.546 = f32[128,128]{1,0:T(8,128)S(1)} custom-call(f32[128,128]{1,0:T(8,128)S(1)} %cholesky.609), custom_call_target="Cholesky" | custom-call | tf_op jit(solution)/shard_map/jit(cholesky)/cholesky | solution.py:45
  496.5 9.8 %custom-call.70 = f32[1,128,128]{1,2,0:T(8,128)S(1)} custom-call(f32[1,128,128]{2,1,0:T(8,128)S(1)} %get-tuple-element.57), custom_call_target="InvertDiagBlocksLowerTriangular" | custom-call | tf_op jit(solution)/shard_map/jit(cholesky)/cholesky | solution.py:45
  509.0 11.7 %cholesky.564 = f32[128,128]{1,0:T(8,128)S(1)} custom-call(f32[128,128]{1,0:T(8,128)S(1)} %convolution_subtract_fusion.6), custom_call_target="Cholesky" | custom-call | tf_op jit(solution)/shard_map/jit(cholesky)/cholesky | solution.py:45
  531.6 4.9 select_select_fusion
  536.5 22.4 %while.1 = (s32[]{:T(128)}, f32[1024,1024]{1,0:T(8,128)}, s32[8,2]{0,1:T(2,128)S(1)}, f32[8,128,128]{2,1,0:T(8,128)S(1)}, s32[]{:T(128)}) while((s32[]{:T(128)}, f32[1024,1024]{1,0:T(8,128)}, s32[8,2]{0,1:T(2,128)S(1)}, f32[8,128,128]{2,1,0:T(8,128)S(1)}, s32[]{:T(128)}) %tuple.76), condition=%wide.while_cond, body=%wide.while_body.sunk | while | flops 2 | bytes 131181 | solution.py:47
  558.9 78.8 %custom-call.71 = f32[8,128,128]{1,2,0:T(8,128)S(1)} custom-call(f32[8,128,128]{2,1,0:T(8,128)S(1)} %get-tuple-element.12), custom_call_target="InvertDiagBlocksLowerTriangular" | custom-call | tf_op jit(solution)/shard_map/triangular_solve | solution.py:47
  660.1 25.5 %convolution_add_fusion = f32[64,8192]{1,0:T(8,128)} fusion(f32[64,8192]{1,0:T(8,128)S(1)} %copy-done, f32[1024,64]{0,1:T(8,128)S(1)} %constant_dynamic-update-slice_fusion.36, f32[1024,8192]{1,0:T(8,128)} %all-gather.8.cloned.1.call-done), kind=kOutput, calls=%fused_computation.2 | convolution fusion | flops 6442975232 | bytes 38010880 | tf_op jit(solution)/shard_map/kj,kc->jc/dot_general | solution.py:98
  (157 shorter events, 90.9 us)
Async XLA Ops:
  6.5 174.3 %all-gather.4.cloned.1.call-start = ((), (), s32[]{:S(2)}) async-start(), calls=%async_computation | async-start | bytes 8912896 | tf_op jit(solution)/shard_map/all_gather | solution.py:91
  24.5 72.8 %copy-start.2 = (f32[2048]{0:T(1024)S(1)}, f32[2048]{0:T(1024)}, u32[]{:S(2)}) copy-start(f32[2048]{0:T(1024)} %param.20) | copy-start | bytes 24580
  24.5 72.8 %copy-start.3 = (f32[2048]{0:T(1024)S(1)}, f32[2048]{0:T(1024)}, u32[]{:S(2)}) copy-start(f32[2048]{0:T(1024)} %param.19) | copy-start | bytes 24580
  99.3 159.0 %all-reduce.4.cloned.1.call-start = ((), (), s32[]{:S(2)}) async-start(), calls=%async_computation.1 | async-start | bytes 1048576 | tf_op jit(solution)/shard_map/psum | solution.py:92
  180.8 79.4 %copy-start = (f32[64,8192]{1,0:T(8,128)S(1)}, f32[64,8192]{1,0:T(8,128)}, u32[]{:S(2)}) copy-start(f32[64,8192]{1,0:T(8,128)} %param.11) | copy-start | bytes 6291460
  192.8 116.3 %all-gather.6.cloned.1.call-start = ((), (), s32[]{:S(2)}) async-start(), calls=%async_computation.2 | async-start | bytes 4456448 | tf_op jit(solution)/shard_map/all_gather | solution.py:93
  260.1 399.9 %all-gather.8.cloned.1.call-start = ((), (), s32[]{:S(2)}) async-start(), calls=%async_computation.3 | async-start | bytes 35651584 | tf_op jit(solution)/shard_map/all_gather | solution.py:101
  325.6 2.0 copy-start.1
Sparse Core Ops, SparseCore 0:
  99.4 81.3 all-gather.3
  192.9 58.3 all-reduce.3
  260.2 48.8 all-gather.5
  311.3 197.7 all-gather.7
where the time goes:
time: 701 us; the launch traced here: 692 us
  other arithmetic  282 us (40%)
  waiting for transfers between devices  129 us (18%)
  blocking collectives  127 us (18%)
  matrix products  92.4 us (13%)
  local copies, waits for them, and re-layouts  41.4 us (6%)
  between operations  20.1 us (3%)
    another operation x30, other arithmetic, spd_solve(): factor = jnp.linalg.cholesky(matrix)  173 us
    another operation x3, other arithmetic, spd_solve(): lax.linalg.triangular_solve(factor, halfway, left_side=True, lower=True,...  83.7 us
    all_gather x1, waiting for transfers between devices, body(): lax.all_gather(pred_anomaly, 'mem', axis=0, tiled=True)  81.4 us
    psum x1, blocking collectives, body(): misfit_sum = lax.psum(misfit_local, ('mem', 'cell'))  64.7 us
    psum x1, blocking collectives, body(): lax.psum((jnp.sum(turnover_effect, axis=0), jnp.sum(predicted, axis=0)),...  62.6 us
    all_gather x1, waiting for transfers between devices, body(): gram = lax.all_gather(summed[:, :local_members], 'mem', axis=1, tiled=True)  47.4 us
    dot_general x1, matrix products, body(): jnp.einsum('kj,kc->jc', local_solve, lax.all_gather(anomaly, 'mem', axis=...  25.5 us
    another operation x14, matrix products, spd_solve(): factor = jnp.linalg.cholesky(matrix)  23.2 us
  transfers between devices with their start and end apart: 4, of which 2 were waited for; matrix products, arithmetic and copies ran while one was open for 50% of the time, Pallas kernels for 0%

commit v1 on v0

--- a/solution.py
+++ b/solution.py
@@ -88,7 +88,34 @@
     stacked = jnp.concatenate(
         [pred_anomaly / obs_var[None, :], departure / obs_var[None, :]], axis=0
     )
-    partial_cols = contract_last(lax.all_gather(pred_anomaly, "mem", axis=0, tiled=True), stacked)
+
+    def _edit_routes_all(axis_no, along_axis, inputs):
+        h_now = lax.axis_size(along_axis)
+        step_out = lax.axis_index(along_axis)
+        t_next, item_now, out_arr = (h_now, step_out, inputs.shape[axis_no])
+        placed = jnp.zeros(
+            [i0 * t_next if dd == axis_no else i0 for dd, i0 in enumerate(inputs.shape)],
+            inputs.dtype,
+        )
+        tall = left_arr = inputs
+        pp = 1
+        q_next = lax.dynamic_update_slice_in_dim(placed, inputs, item_now * out_arr, axis=axis_no)
+        while pp < t_next // 2 + 1:
+            tall = lax.ppermute(tall, along_axis, [(dd, (dd + 1) % t_next) for dd in range(t_next)])
+            q_next = lax.dynamic_update_slice_in_dim(
+                q_next, tall, (item_now - pp) % t_next * out_arr, axis=axis_no
+            )
+            if 2 * pp < t_next:
+                left_arr = lax.ppermute(
+                    left_arr, along_axis, [(dd, (dd - 1) % t_next) for dd in range(t_next)]
+                )
+                q_next = lax.dynamic_update_slice_in_dim(
+                    q_next, left_arr, (item_now + pp) % t_next * out_arr, axis=axis_no
+                )
+            pp += 1
+        return q_next
+
+    partial_cols = contract_last(_edit_routes_all(0, "mem", pred_anomaly), stacked)
     summed = lax.psum(partial_cols, "cell")
     gram = lax.all_gather(summed[:, :local_members], "mem", axis=1, tiled=True)
     step_size = member_count * all_obs / misfit_sum

time: 701 us -> 742 us (1.058)
  starting transfers between devices: 0.13 us -> 35.7 us
  waiting for transfers between devices: 129 us -> 98.7 us
  local copies, waits for them, and re-layouts: 41.4 us -> 62.3 us
  blocking collectives: 127 us -> 142 us
    all_gather x1 -> x0, waiting for transfers between devices: 81.4 us -> none  [body(): lax.all_gather(pred_anomaly, 'mem', axis=0, tiled=True)]
    ppermute x0 -> x15, waiting for transfers between devices: none -> 51.2 us  [the longest x8 28.1 us: _edit_routes_all(): lax.ppermute(tall, along_axis, [(dd, (dd + 1) % t_next) for dd in range(t...]
    ppermute x0 -> x15, starting transfers between devices: none -> 35.6 us  [the longest x7 35.4 us: _edit_routes_all(): lax.ppermute(left_arr, along_axis, [(dd, (dd - 1) % t_next) for dd in ran...]
    dynamic_update_slice x0 -> x16, local copies, waits for them, and re-layouts: none -> 17.7 us  [the longest x8 8.84 us: _edit_routes_all(): lax.dynamic_update_slice_in_dim(q_next, tall, (item_now - pp) % t_next *...]
    psum x1, blocking collectives: 64.7 us -> 79.7 us  [body(): misfit_sum = lax.psum(misfit_local, ('mem', 'cell'))]
  transfers between devices with their start and end apart: 4 -> 18, of which waited for: 2 -> 9; matrix products, arithmetic and copies ran while one was open for 50% -> 50% of each run, Pallas kernels for 0% -> 0%
where the time goes in v1:
time: 742 us; the launch traced here: 732 us
  other arithmetic  280 us (38%)
  blocking collectives  142 us (19%)
  waiting for transfers between devices  98.7 us (13%)
  matrix products  92.4 us (12%)
  local copies, waits for them, and re-layouts  62.3 us (8%)
  starting transfers between devices  35.7 us (5%)
  between operations  20.1 us (3%)
    another operation x30, other arithmetic, spd_solve(): factor = jnp.linalg.cholesky(matrix)  173 us
    another operation x3, other arithmetic, spd_solve(): lax.linalg.triangular_solve(factor, halfway, left_side=True, lower=True,...  83.7 us
    psum x1, blocking collectives, body(): misfit_sum = lax.psum(misfit_local, ('mem', 'cell'))  79.7 us
    psum x1, blocking collectives, body(): lax.psum((jnp.sum(turnover_effect, axis=0), jnp.sum(predicted, axis=0)),...  62.6 us
    all_gather x1, waiting for transfers between devices, body(): gram = lax.all_gather(summed[:, :local_members], 'mem', axis=1, tiled=True)  47.4 us
    ppermute x7, starting transfers between devices, _edit_routes_all(): lax.ppermute(left_arr, along_axis, [(dd, (dd - 1) % t_next) for dd in ran...  35.4 us
    ppermute x8, waiting for transfers between devices, _edit_routes_all(): lax.ppermute(tall, along_axis, [(dd, (dd + 1) % t_next) for dd in range(t...  28.1 us
    dot_general x1, matrix products, body(): jnp.einsum('kj,kc->jc', local_solve, lax.all_gather(anomaly, 'mem', axis=...  25.5 us
  transfers between devices with their start and end apart: 18, of which 9 were waited for; matrix products, arithmetic and copies ran while one was open for 50% of the time, Pallas kernels for 0%

profile of v1, /device:TPU:1, one launch (start us, length us, event | category | flops | bytes accessed | tf_op | source)
XLA Modules:
  0.0 732.1 jit_solution(17211580333655776428)
XLA Ops:
  16.6 7.3 fusion.138
  23.9 9.8 %fusion.32 = (f32[]{:T(128)}, f32[64,32]{1,0:T(8,128)S(1)}, f32[64,32,64]{2,1,0:T(8,128)S(1)}) fusion(f32[64,32]{1,0:T(8,128)S(1)} %div.48, f32[64,32]{1,0:T(8,128)S(1)} %sub.108, f32[8,64,8,128]{3,2,1,0:T(8,128)S(1)} %get-tuple-element.42, f32[64,32]{1,0:T(8,128)S(1)} %mul.316, s32[64,32]{1,0:T(8,128)S(1)} %eq.96, f32[64,32]{1,0:T(8,128)S(1)} %mul.313, ...), kind=kOutput, calls=%fused_computation.81 | convolution fusion | flops 204863488 | bytes 2711556 | tf_op jit(solution)/shard_map/jbc,boc->jbo/dot_general | solution.py:40
  33.8 62.6 %all-reduce.1 = (f32[2048]{0:T(1024)S(1)}, f32[8192]{0:T(1024)S(1)}) all-reduce(f32[2048]{0:T(1024)S(1)} %reduce_sum.31, f32[8192]{0:T(1024)S(1)} %get-tuple-element.41), channel_id=1, replica_groups=mesh['mem'=16,'cell'=8] {'mem'}, use_global_device_ids=true, to_apply=%region_3.0 | all-reduce | flops 10240 | bytes 81920 | tf_op jit(solution)/shard_map/psum | solution.py:78
  101.8 6.6 collective-permute-done
  113.2 8.4 %collective-permute-done.2 = f32[64,2048]{1,0:T(8,128)S(1)} collective-permute-done((f32[64,2048]{1,0:T(8,128)S(1)}, f32[64,2048]{1,0:T(8,128)S(1)}, u32[]{:S(2)}, u32[]{:S(2)}) %collective-permute-start.2) | collective-permute-done | bytes 524320 | tf_op jit(solution)/shard_map/ppermute | solution.py:104
  126.4 7.5 %collective-permute-done.4 = f32[64,2048]{1,0:T(8,128)S(1)} collective-permute-done((f32[64,2048]{1,0:T(8,128)S(1)}, f32[64,2048]{1,0:T(8,128)S(1)}, u32[]{:S(2)}, u32[]{:S(2)}) %collective-permute-start.4) | collective-permute-done | bytes 524320 | tf_op jit(solution)/shard_map/ppermute | solution.py:104
  150.3 6.5 collective-permute-done.7
  165.6 5.8 collective-permute-done.9
  179.5 5.9 collective-permute-done.11
  199.3 5.6 collective-permute-done.14
  205.7 12.0 %fusion.19 = f32[1024,128]{0,1:T(8,128)} fusion(f32[1024,2048]{1,0:T(8,128)} %constant_dynamic-update-slice_fusion.44, f32[64,2048]{1,0:T(8,128)S(1)} %get-tuple-element.43, f32[64,2048]{1,0:T(8,128)S(1)} %get-tuple-element.33), kind=kOutput, calls=%fused_computation.62 | convolution fusion | flops 3221487616 | bytes 9961472 | tf_op jit(solution)/shard_map/dot_general | solution.py:53
  217.8 79.7 %psum.28 = f32[]{:T(128)} all-reduce(f32[]{:T(128)} %get-tuple-element.13), channel_id=1, replica_groups=mesh['mem'=16,'cell'=8] {'mem','cell'}, use_global_device_ids=true, to_apply=%region_1.0 | all-reduce | flops 1 | bytes 8 | tf_op jit(solution)/shard_map/psum | solution.py:87
  301.7 47.4 %all-gather.3.cloned.1.call-done = f32[1024,1024]{0,1:T(8,128)} async-done(((f32[1024,64]{0,1:T(8,128)}), f32[1024,1024]{0,1:T(8,128)}) %all-gather.3.cloned.1.call-update) | async-done | bytes 4194320 | tf_op jit(solution)/shard_map/all_gather | solution.py:120
  359.3 5.8 fusion
  367.2 11.7 %cholesky.223 = f32[128,128]{1,0:T(8,128)S(1)} custom-call(f32[128,128]{1,0:T(8,128)S(1)} %cholesky.580), custom_call_target="Cholesky" | custom-call | tf_op jit(solution)/shard_map/jit(cholesky)/cholesky | solution.py:45
  381.4 9.8 %custom-call.64 = f32[1,128,128]{1,2,0:T(8,128)S(1)} custom-call(f32[1,128,128]{2,1,0:T(8,128)S(1)} %get-tuple-element.75), custom_call_target="InvertDiagBlocksLowerTriangular" | custom-call | tf_op jit(solution)/shard_map/jit(cholesky)/cholesky | solution.py:45
  395.2 12.1 %cholesky.244 = f32[128,128]{1,0:T(8,128)S(1)} custom-call(f32[128,128]{1,0:T(8,128)S(1)} %cholesky.584), custom_call_target="Cholesky" | custom-call | tf_op jit(solution)/shard_map/jit(cholesky)/cholesky | solution.py:45
  407.9 9.8 %custom-call.65 = f32[1,128,128]{1,2,0:T(8,128)S(1)} custom-call(f32[1,128,128]{2,1,0:T(8,128)S(1)} %get-tuple-element.72), custom_call_target="InvertDiagBlocksLowerTriangular" | custom-call | tf_op jit(solution)/shard_map/jit(cholesky)/cholesky | solution.py:45
  421.1 11.7 %cholesky.468 = f32[128,128]{1,0:T(8,128)S(1)} custom-call(f32[128,128]{1,0:T(8,128)S(1)} %cholesky.589), custom_call_target="Cholesky" | custom-call | tf_op jit(solution)/shard_map/jit(cholesky)/cholesky | solution.py:45
  433.5 9.8 %custom-call.66 = f32[1,128,128]{1,2,0:T(8,128)S(1)} custom-call(f32[1,128,128]{2,1,0:T(8,128)S(1)} %get-tuple-element.69), custom_call_target="InvertDiagBlocksLowerTriangular" | custom-call | tf_op jit(solution)/shard_map/jit(cholesky)/cholesky | solution.py:45
  446.8 11.9 %cholesky.487 = f32[128,128]{1,0:T(8,128)S(1)} custom-call(f32[128,128]{1,0:T(8,128)S(1)} %cholesky.594), custom_call_target="Cholesky" | custom-call | tf_op jit(solution)/shard_map/jit(cholesky)/cholesky | solution.py:45
  459.3 9.8 %custom-call.67 = f32[1,128,128]{1,2,0:T(8,128)S(1)} custom-call(f32[1,128,128]{2,1,0:T(8,128)S(1)} %get-tuple-element.66), custom_call_target="InvertDiagBlocksLowerTriangular" | custom-call | tf_op jit(solution)/shard_map/jit(cholesky)/cholesky | solution.py:45
  472.6 11.7 %cholesky.506 = f32[128,128]{1,0:T(8,128)S(1)} custom-call(f32[128,128]{1,0:T(8,128)S(1)} %cholesky.599), custom_call_target="Cholesky" | custom-call | tf_op jit(solution)/shard_map/jit(cholesky)/cholesky | solution.py:45
  485.0 10.0 %custom-call.68 = f32[1,128,128]{1,2,0:T(8,128)S(1)} custom-call(f32[1,128,128]{2,1,0:T(8,128)S(1)} %get-tuple-element.63), custom_call_target="InvertDiagBlocksLowerTriangular" | custom-call | tf_op jit(solution)/shard_map/jit(cholesky)/cholesky | solution.py:45
  498.4 11.7 %cholesky.526 = f32[128,128]{1,0:T(8,128)S(1)} custom-call(f32[128,128]{1,0:T(8,128)S(1)} %cholesky.604), custom_call_target="Cholesky" | custom-call | tf_op jit(solution)/shard_map/jit(cholesky)/cholesky | solution.py:45
  510.7 9.8 %custom-call.69 = f32[1,128,128]{1,2,0:T(8,128)S(1)} custom-call(f32[1,128,128]{2,1,0:T(8,128)S(1)} %get-tuple-element.60), custom_call_target="InvertDiagBlocksLowerTriangular" | custom-call | tf_op jit(solution)/shard_map/jit(cholesky)/cholesky | solution.py:45
  523.5 12.1 %cholesky.546 = f32[128,128]{1,0:T(8,128)S(1)} custom-call(f32[128,128]{1,0:T(8,128)S(1)} %cholesky.609), custom_call_target="Cholesky" | custom-call | tf_op jit(solution)/shard_map/jit(cholesky)/cholesky | solution.py:45
  536.3 9.8 %custom-call.70 = f32[1,128,128]{1,2,0:T(8,128)S(1)} custom-call(f32[1,128,128]{2,1,0:T(8,128)S(1)} %get-tuple-element.57), custom_call_target="InvertDiagBlocksLowerTriangular" | custom-call | tf_op jit(solution)/shard_map/jit(cholesky)/cholesky | solution.py:45
  548.8 11.7 %cholesky.564 = f32[128,128]{1,0:T(8,128)S(1)} custom-call(f32[128,128]{1,0:T(8,128)S(1)} %convolution_subtract_fusion.6), custom_call_target="Cholesky" | custom-call | tf_op jit(solution)/shard_map/jit(cholesky)/cholesky | solution.py:45
  576.3 22.4 %while.1 = (s32[]{:T(128)}, f32[1024,1024]{1,0:T(8,128)}, s32[8,2]{0,1:T(2,128)S(1)}, f32[8,128,128]{2,1,0:T(8,128)S(1)}, s32[]{:T(128)}) while((s32[]{:T(128)}, f32[1024,1024]{1,0:T(8,128)}, s32[8,2]{0,1:T(2,128)S(1)}, f32[8,128,128]{2,1,0:T(8,128)S(1)}, s32[]{:T(128)}) %tuple.76), condition=%wide.while_cond, body=%wide.while_body.sunk | while | flops 2 | bytes 131181 | solution.py:47
  598.7 78.8 %custom-call.71 = f32[8,128,128]{1,2,0:T(8,128)S(1)} custom-call(f32[8,128,128]{2,1,0:T(8,128)S(1)} %get-tuple-element.12), custom_call_target="InvertDiagBlocksLowerTriangular" | custom-call | tf_op jit(solution)/shard_map/triangular_solve | solution.py:47
  699.8 25.5 %convolution_add_fusion = f32[64,8192]{1,0:T(8,128)} fusion(f32[64,8192]{1,0:T(8,128)S(1)} %copy-done, f32[1024,64]{0,1:T(8,128)S(1)} %constant_dynamic-update-slice_fusion.36, f32[1024,8192]{1,0:T(8,128)} %all-gather.5.cloned.1.call-done), kind=kOutput, calls=%fused_computation.2 | convolution fusion | flops 6442975232 | bytes 38010880 | tf_op jit(solution)/shard_map/kj,kc->jc/dot_general | solution.py:125
  (207 shorter events, 173.3 us)
Async XLA Ops:
  6.5 291.7 %all-reduce.4.cloned.1.call-start = ((), (), s32[]{:S(2)}) async-start(), calls=%async_computation | async-start | bytes 1048576 | tf_op jit(solution)/shard_map/psum | solution.py:119
  23.9 72.8 %copy-start.4 = (f32[64,2048]{1,0:T(8,128)S(1)}, f32[64,2048]{1,0:T(8,128)}, u32[]{:S(2)}) copy-start(f32[64,2048]{1,0:T(8,128)} %param.21) | copy-start | bytes 1572868
  23.9 72.8 %copy-start.5 = (f32[2048]{0:T(1024)S(1)}, f32[2048]{0:T(1024)}, u32[]{:S(2)}) copy-start(f32[2048]{0:T(1024)} %param.20) | copy-start | bytes 24580
  23.9 72.8 %copy-start.6 = (f32[2048]{0:T(1024)S(1)}, f32[2048]{0:T(1024)}, u32[]{:S(2)}) copy-start(f32[2048]{0:T(1024)} %param.19) | copy-start | bytes 24580
  96.9 11.5 %collective-permute-start = (f32[64,2048]{1,0:T(8,128)S(1)}, f32[64,2048]{1,0:T(8,128)S(1)}, u32[]{:S(2)}, u32[]{:S(2)}) collective-permute-start(f32[64,2048]{1,0:T(8,128)S(1)} %get-tuple-element.34), channel_id=1, source_target_pairs={{0,8},{8,16},{16,24},{24,32},{32,40},{40,48},{48,56},{56,64},{64,7... | collective-permute-start | bytes 1572872 | tf_op jit(solution)/shard_map/ppermute | solution.py:104
  97.0 11.4 %collective-permute-start.1 = (f32[64,2048]{1,0:T(8,128)S(1)}, f32[64,2048]{1,0:T(8,128)S(1)}, u32[]{:S(2)}, u32[]{:S(2)}) collective-permute-start(f32[64,2048]{1,0:T(8,128)S(1)} %get-tuple-element.34), channel_id=1, source_target_pairs={{0,120},{8,0},{16,8},{24,16},{32,24},{40,32},{48,40},{56,48},{64,5... | collective-permute-start | bytes 1572872 | tf_op jit(solution)/shard_map/ppermute | solution.py:109
  108.4 4.8 copy-start.3
  108.4 13.2 %collective-permute-start.2 = (f32[64,2048]{1,0:T(8,128)S(1)}, f32[64,2048]{1,0:T(8,128)S(1)}, u32[]{:S(2)}, u32[]{:S(2)}) collective-permute-start(f32[64,2048]{1,0:T(8,128)S(1)} %collective-permute-done), channel_id=1, source_target_pairs={{0,8},{8,16},{16,24},{24,32},{32,40},{40,48},{48,56},{56,64},{64,7... | collective-permute-start | bytes 1572872 | tf_op jit(solution)/shard_map/ppermute | solution.py:104
  108.4 13.2 %copy-start.2 = (f32[64,2048]{1,0:T(8,128)}, f32[64,2048]{1,0:T(8,128)S(1)}, u32[]{:S(2)}) copy-start(f32[64,2048]{1,0:T(8,128)S(1)} %collective-permute-done.1) | copy-start | bytes 1572868
  108.4 13.2 %collective-permute-start.3 = (f32[64,2048]{1,0:T(8,128)S(1)}, f32[64,2048]{1,0:T(8,128)}, u32[]{:S(2)}, u32[]{:S(2)}) collective-permute-start(f32[64,2048]{1,0:T(8,128)S(1)} %collective-permute-done.1), channel_id=1, source_target_pairs={{0,120},{8,0},{16,8},{24,16},{32,24},{40,32},{48,40},{56,48},{64,5... | collective-permute-start | bytes 1572872 | tf_op jit(solution)/shard_map/ppermute | solution.py:109
  121.6 12.3 %collective-permute-start.4 = (f32[64,2048]{1,0:T(8,128)S(1)}, f32[64,2048]{1,0:T(8,128)S(1)}, u32[]{:S(2)}, u32[]{:S(2)}) collective-permute-start(f32[64,2048]{1,0:T(8,128)S(1)} %collective-permute-done.2), channel_id=1, source_target_pairs={{0,8},{8,16},{16,24},{24,32},{32,40},{40,48},{48,56},{56,64},{64,7... | collective-permute-start | bytes 1572872 | tf_op jit(solution)/shard_map/ppermute | solution.py:104
  121.6 19.3 %collective-permute-start.5 = (f32[64,2048]{1,0:T(8,128)}, f32[64,2048]{1,0:T(8,128)S(1)}, u32[]{:S(2)}, u32[]{:S(2)}) collective-permute-start(f32[64,2048]{1,0:T(8,128)} %collective-permute-done.3), channel_id=1, source_target_pairs={{0,120},{8,0},{16,8},{24,16},{32,24},{40,32},{48,40},{56,48},{64,5... | collective-permute-start | bytes 1572872 | tf_op jit(solution)/shard_map/ppermute | solution.py:109
  133.9 13.7 %collective-permute-start.6 = (f32[64,2048]{1,0:T(8,128)S(1)}, f32[64,2048]{1,0:T(8,128)}, u32[]{:S(2)}, u32[]{:S(2)}) collective-permute-start(f32[64,2048]{1,0:T(8,128)S(1)} %collective-permute-done.4), channel_id=1, source_target_pairs={{0,8},{8,16},{16,24},{24,32},{32,40},{40,48},{48,56},{56,64},{64,7... | collective-permute-start | bytes 1572872 | tf_op jit(solution)/shard_map/ppermute | solution.py:104
  140.9 15.9 %collective-permute-start.7 = (f32[64,2048]{1,0:T(8,128)S(1)}, f32[64,2048]{1,0:T(8,128)S(1)}, u32[]{:S(2)}, u32[]{:S(2)}) collective-permute-start(f32[64,2048]{1,0:T(8,128)S(1)} %collective-permute-done.5), channel_id=1, source_target_pairs={{0,120},{8,0},{16,8},{24,16},{32,24},{40,32},{48,40},{56,48},{64,5... | collective-permute-start | bytes 1572872 | tf_op jit(solution)/shard_map/ppermute | solution.py:109
  147.5 15.3 %collective-permute-start.8 = (f32[64,2048]{1,0:T(8,128)}, f32[64,2048]{1,0:T(8,128)S(1)}, u32[]{:S(2)}, u32[]{:S(2)}) collective-permute-start(f32[64,2048]{1,0:T(8,128)} %collective-permute-done.6), channel_id=1, source_target_pairs={{0,8},{8,16},{16,24},{24,32},{32,40},{40,48},{48,56},{56,64},{64,7... | collective-permute-start | bytes 1572872 | tf_op jit(solution)/shard_map/ppermute | solution.py:104
  156.8 14.6 %collective-permute-start.9 = (f32[64,2048]{1,0:T(8,128)S(1)}, f32[64,2048]{1,0:T(8,128)S(1)}, u32[]{:S(2)}, u32[]{:S(2)}) collective-permute-start(f32[64,2048]{1,0:T(8,128)S(1)} %collective-permute-done.7), channel_id=1, source_target_pairs={{0,120},{8,0},{16,8},{24,16},{32,24},{40,32},{48,40},{56,48},{64,5... | collective-permute-start | bytes 1572872 | tf_op jit(solution)/shard_map/ppermute | solution.py:109
  162.9 14.9 %collective-permute-start.10 = (f32[64,2048]{1,0:T(8,128)S(1)}, f32[64,2048]{1,0:T(8,128)S(1)}, u32[]{:S(2)}, u32[]{:S(2)}) collective-permute-start(f32[64,2048]{1,0:T(8,128)S(1)} %collective-permute-done.8), channel_id=1, source_target_pairs={{0,8},{8,16},{16,24},{24,32},{32,40},{40,48},{48,56},{56,64},{64,7... | collective-permute-start | bytes 1572872 | tf_op jit(solution)/shard_map/ppermute | solution.py:104
  171.4 14.0 %collective-permute-start.11 = (f32[64,2048]{1,0:T(8,128)S(1)}, f32[64,2048]{1,0:T(8,128)S(1)}, u32[]{:S(2)}, u32[]{:S(2)}) collective-permute-start(f32[64,2048]{1,0:T(8,128)S(1)} %collective-permute-done.9), channel_id=1, source_target_pairs={{0,120},{8,0},{16,8},{24,16},{32,24},{40,32},{48,40},{56,48},{64,5... | collective-permute-start | bytes 1572872 | tf_op jit(solution)/shard_map/ppermute | solution.py:109
  177.8 14.0 %collective-permute-start.12 = (f32[64,2048]{1,0:T(8,128)S(1)}, f32[64,2048]{1,0:T(8,128)S(1)}, u32[]{:S(2)}, u32[]{:S(2)}) collective-permute-start(f32[64,2048]{1,0:T(8,128)S(1)} %collective-permute-done.10), channel_id=1, source_target_pairs={{0,8},{8,16},{16,24},{24,32},{32,40},{40,48},{48,56},{56,64},{64,7... | collective-permute-start | bytes 1572872 | tf_op jit(solution)/shard_map/ppermute | solution.py:104
  185.4 13.1 %collective-permute-start.13 = (f32[64,2048]{1,0:T(8,128)S(1)}, f32[64,2048]{1,0:T(8,128)S(1)}, u32[]{:S(2)}, u32[]{:S(2)}) collective-permute-start(f32[64,2048]{1,0:T(8,128)S(1)} %collective-permute-done.11), channel_id=1, source_target_pairs={{0,120},{8,0},{16,8},{24,16},{32,24},{40,32},{48,40},{56,48},{64,5... | collective-permute-start | bytes 1572872 | tf_op jit(solution)/shard_map/ppermute | solution.py:109
  191.8 13.1 %collective-permute-start.14 = (f32[64,2048]{1,0:T(8,128)S(1)}, f32[64,2048]{1,0:T(8,128)S(1)}, u32[]{:S(2)}, u32[]{:S(2)}) collective-permute-start(f32[64,2048]{1,0:T(8,128)S(1)} %collective-permute-done.12), channel_id=1, source_target_pairs={{0,8},{8,16},{16,24},{24,32},{32,40},{40,48},{48,56},{56,64},{64,7... | collective-permute-start | bytes 1572872 | tf_op jit(solution)/shard_map/ppermute | solution.py:104
  205.7 94.4 %copy-start = (f32[64,8192]{1,0:T(8,128)S(1)}, f32[64,8192]{1,0:T(8,128)}, u32[]{:S(2)}) copy-start(f32[64,8192]{1,0:T(8,128)} %param.11) | copy-start | bytes 6291460
  217.7 131.3 %all-gather.3.cloned.1.call-start = ((), (), s32[]{:S(2)}) async-start(), calls=%async_computation.1 | async-start | bytes 4456448 | tf_op jit(solution)/shard_map/all_gather | solution.py:120
  300.0 399.8 %all-gather.5.cloned.1.call-start = ((), (), s32[]{:S(2)}) async-start(), calls=%async_computation.2 | async-start | bytes 35651584 | tf_op jit(solution)/shard_map/all_gather | solution.py:128
  365.2 2.0 copy-start.1
Sparse Core Ops, SparseCore 0:
  217.9 71.6 all-reduce.3
  300.2 48.8 all-gather.2
  351.4 197.1 all-gather.4
